TPU v7x, 256 devices: a whole 4x4x8 slice. The times are simulated.
256 devices in a mesh: row: 8 (over x, core), col: 32 (over y, z).
Axes of the slice: x: 4, y: 4, z: 8, core: 2. Of those that a mesh axis runs over, the one named last changes fastest.
Arguments:
- factor: float32 [6, 8, 32, 512, 512], P(None, 'row', 'col'), may hold values from -0.1875 to 0.1875
- rhs: float32 [6, 8, 32, 128, 128], P(None, 'row', 'col'), may hold values from -6 to 6
- inverses: float32 [4, 512, 512], replicated, may hold values from -0.5 to 2, as said below
Outputs:
- solved: float32 [4, 512, 128], P(None, 'col')
- remaining: float32 [6, 8, 32, 128, 128], P(None, 'row', 'col')
Inputs may be any that keep to these rules, and one draw needn't show every extreme that they name: `inverses`: each block is lower triangular with its diagonal between 0.5 and 2 and entries below it of magnitude at most 4 / sqrt(512).
All inputs are finite; a program needn't handle non-finite values.
Results may differ from a plain program's by a relative error of at most 0.00011.
Values sent between devices are 32-bit elements; how exact they have to be, the bound alone decides.
A program may use at most 64 MiB of HBM per device.

v0:
```python
import jax
import jax.numpy as jnp
from jax import lax
from jax.sharding import PartitionSpec as P


def shifted(block, axis, distance):
    devices = range(lax.axis_size(axis))
    route = [((i - distance) % len(devices), i) for i in devices]
    return lax.ppermute(block, axis, route)


def broadcast(x, axis, root):
    mine = lax.axis_index(axis) == root
    return lax.psum(jnp.where(mine, x, jnp.zeros_like(x)), axis)


def group_reduce(update, member, steps, groups):
    blocks = update.shape[0]
    nrhs = update.shape[2]
    split = update.reshape(blocks, steps, update.shape[1] // steps, nrhs)
    total = lax.dynamic_index_in_dim(split, member, 1, keepdims=False)
    for offset in range(1, steps):
        piece = lax.dynamic_index_in_dim(split, (member + offset) % steps, 1, keepdims=False)
        total = total + shifted(piece, "col", offset * groups)
    return total


def on_device(factor, rhs, inverses):
    steps = inverses.shape[0]
    blocks = factor.shape[0]
    width = factor.shape[3]
    quarter = rhs.shape[3]
    nrhs = rhs.shape[4]
    row_count = lax.axis_size("row")
    col_count = lax.axis_size("col")
    groups = col_count // steps
    row_pos = lax.axis_index("row")
    col_pos = lax.axis_index("col")
    member = col_pos // groups
    group = col_pos % groups
    block_ids = (jnp.arange(blocks, dtype=jnp.int32) * row_count + row_pos) * groups + group
    panel = factor[:, 0, 0]
    current = rhs[:, 0, 0]
    solved_list = []
    for k in range(steps):
        owner_row = k // groups
        owner_group = k % groups
        placed = lax.dynamic_update_slice(
            jnp.zeros((width, nrhs), jnp.float32),
            current[0],
            (member * quarter, jnp.zeros((), jnp.int32)),
        )
        contrib = placed
        is_owner = jnp.logical_and(row_pos == owner_row, group == owner_group)
        contrib = jnp.where(is_owner, contrib, jnp.zeros_like(contrib))
        complete = lax.psum(contrib, "col")
        solved_block = jnp.dot(inverses[k], complete, precision=lax.Precision.HIGHEST)
        solved_block = broadcast(solved_block, "row", owner_row)
        solved_list.append(solved_block)
        keep = (block_ids > k).astype(jnp.float32)[:, None, None]

        def column_update(solved_now=solved_block, keep_now=keep):
            return (
                jnp.einsum("rji,jh->rih", panel, solved_now, precision=lax.Precision.HIGHEST)
                * keep_now
            )

        def no_update():
            return jnp.zeros((blocks, width, nrhs), jnp.float32)

        update = lax.cond(member == k, column_update, no_update)
        current = current - group_reduce(update, member, steps, groups)
    stacked = jnp.stack(solved_list)
    share = width // col_count
    solved_rows = lax.dynamic_slice_in_dim(stacked, col_pos * share, share, 1)
    return (solved_rows, current[:, None, None])


def solution(mesh):
    in_specs = (P(None, "row", "col", None, None), P(None, "row", "col", None, None), P())
    out_specs = (P(None, "col", None), P(None, "row", "col", None, None))
    return jax.shard_map(
        on_device, mesh=mesh, in_specs=in_specs, out_specs=out_specs, check_vma=False
    )
```

profile of v0, /device:TPU:7, one launch (start us, length us, event | category | flops | bytes accessed | tf_op | source)
XLA Modules:
  0.0 980.9 jit_solution(4131290574086656395)
XLA Ops:
  9.0 6.6 copy.5
  15.6 139.2 %all-reduce.9.cloned.1.call-done = f32[512,128]{1,0:T(8,128)} async-done(((f32[512,128]{1,0:T(8,128)}), f32[512,128]{1,0:T(8,128)}) %all-reduce.9.cloned.1.call-update) | async-done | bytes 262160 | tf_op jit(solution)/shard_map/psum | solution.py:57
  154.7 3.3 fusion.7
  158.1 65.0 %all-reduce.11.cloned.1.call-done = f32[512,128]{0,1:T(8,128)} async-done(((f32[512,128]{0,1:T(8,128)}), f32[512,128]{0,1:T(8,128)}) %all-reduce.11.cloned.1.call-update) | async-done | bytes 262160 | tf_op jit(solution)/shard_map/psum | solution.py:15
  223.1 7.2 conditional.4
  223.1 7.2 convolution_multiply_fusion
  231.2 2.7 collective-permute-start.2
  233.8 18.1 %collective-permute-done = f32[6,128,128]{2,1,0:T(8,128)S(1)} collective-permute-done((f32[6,128,128]{2,1,0:T(8,128)}, f32[6,128,128]{2,1,0:T(8,128)S(1)}, u32[]{:S(2)}, u32[]{:S(2)}) %collective-permute-start) | collective-permute-done | bytes 393248 | tf_op jit(solution)/shard_map/ppermute | solution.py:10
  252.2 1.1 fusion.28
  254.1 140.4 %all-reduce.13.cloned.1.call-done = f32[512,128]{1,0:T(8,128)} async-done(((f32[512,128]{1,0:T(8,128)}), f32[512,128]{1,0:T(8,128)}) %all-reduce.13.cloned.1.call-update) | async-done | bytes 262160 | tf_op jit(solution)/shard_map/psum | solution.py:57
  394.5 3.3 fusion.6
  397.8 65.0 %all-reduce.15.cloned.1.call-done = f32[512,128]{0,1:T(8,128)} async-done(((f32[512,128]{0,1:T(8,128)}), f32[512,128]{0,1:T(8,128)}) %all-reduce.15.cloned.1.call-update) | async-done | bytes 262160 | tf_op jit(solution)/shard_map/psum | solution.py:15
  463.9 8.2 collective-permute-start.3
  472.1 2.4 collective-permute-start.5
  474.5 6.6 collective-permute-done.3
  481.1 8.3 collective-permute-done.4
  492.2 141.5 %all-reduce.17.cloned.1.call-done = f32[512,128]{1,0:T(8,128)} async-done(((f32[512,128]{1,0:T(8,128)}), f32[512,128]{1,0:T(8,128)}) %all-reduce.17.cloned.1.call-update) | async-done | bytes 262160 | tf_op jit(solution)/shard_map/psum | solution.py:57
  633.7 3.3 fusion.5
  637.0 65.1 %all-reduce.19.cloned.1.call-done = f32[512,128]{0,1:T(8,128)} async-done(((f32[512,128]{0,1:T(8,128)}), f32[512,128]{0,1:T(8,128)}) %all-reduce.19.cloned.1.call-update) | async-done | bytes 262160 | tf_op jit(solution)/shard_map/psum | solution.py:15
  703.1 1.2 collective-permute-start.6
  704.3 8.5 collective-permute-start.7
  712.9 2.1 collective-permute-start.8
  715.4 15.7 %collective-permute-done.7 = f32[6,128,128]{2,1,0:T(8,128)S(1)} collective-permute-done((f32[6,128,128]{2,1,0:T(8,128)S(1)}, f32[6,128,128]{2,1,0:T(8,128)S(1)}, u32[]{:S(2)}, u32[]{:S(2)}) %collective-permute-start.7) | collective-permute-done | bytes 393248 | tf_op jit(solution)/shard_map/ppermute | solution.py:10
  731.1 1.1 fusion.22
  733.0 141.1 %all-reduce.21.cloned.1.call-done = f32[512,128]{1,0:T(8,128)} async-done(((f32[512,128]{1,0:T(8,128)}), f32[512,128]{1,0:T(8,128)}) %all-reduce.21.cloned.1.call-update) | async-done | bytes 262160 | tf_op jit(solution)/shard_map/psum | solution.py:57
  874.1 3.3 fusion.4
  877.4 65.1 %all-reduce.23.cloned.1.call-done = f32[512,128]{0,1:T(8,128)} async-done(((f32[512,128]{0,1:T(8,128)}), f32[512,128]{0,1:T(8,128)}) %all-reduce.23.cloned.1.call-update) | async-done | bytes 262160 | tf_op jit(solution)/shard_map/psum | solution.py:15
  943.8 2.7 collective-permute-start.10
  946.5 6.7 collective-permute-start.11
  954.7 1.8 collective-permute-done.10
  956.5 15.5 %collective-permute-done.11 = f32[6,128,128]{2,1,0:T(8,128)} collective-permute-done((f32[6,128,128]{2,1,0:T(8,128)}, f32[6,128,128]{2,1,0:T(8,128)}, u32[]{:S(2)}, u32[]{:S(2)}) %collective-permute-start.11) | collective-permute-done | bytes 393248 | tf_op jit(solution)/shard_map/ppermute | solution.py:10
  972.0 2.1 fusion.19
  (67 shorter events, 13.0 us)
Async XLA Ops:
  7.2 147.6 %all-reduce.9.cloned.1.call-start = ((), (), s32[]{:S(2)}) async-start(), calls=%async_computation | async-start | bytes 524288 | tf_op jit(solution)/shard_map/psum | solution.py:57
  8.1 0.7 copy-start.5
  8.9 214.3 %all-reduce.11.cloned.1.call-start = ((), (), s32[]{:S(2)}) async-start(), calls=%async_computation.1 | async-start | bytes 524288 | tf_op jit(solution)/shard_map/psum | solution.py:15
  158.0 236.5 %all-reduce.13.cloned.1.call-start = ((), (), s32[]{:S(2)}) async-start(), calls=%async_computation.2 | async-start | bytes 524288 | tf_op jit(solution)/shard_map/psum | solution.py:57
  230.3 21.9 %copy-start.8 = (f32[6,1,1,128,128]{4,3,2,1,0:T(8,128)S(1)}, f32[6,1,1,128,128]{4,3,2,1,0:T(8,128)}, u32[]{:S(2)}) copy-start(f32[6,1,1,128,128]{4,3,2,1,0:T(8,128)} %param.12) | copy-start | bytes 1179652
  231.1 20.7 %collective-permute-start = (f32[6,128,128]{2,1,0:T(8,128)}, f32[6,128,128]{2,1,0:T(8,128)S(1)}, u32[]{:S(2)}, u32[]{:S(2)}) collective-permute-start(f32[6,128,128]{2,1,0:T(8,128)} %get-tuple-element.79), channel_id=1, source_target_pairs={{24,0},{25,1},{26,2},{27,3},{28,4},{29,5},{30,6},{31,7},{0,8},{1,9... | collective-permute-start | bytes 1179656 | tf_op jit(solution)/shard_map/ppermute | solution.py:10
  231.1 20.7 %collective-permute-start.1 = (f32[6,128,128]{2,1,0:T(8,128)S(1)}, f32[6,128,128]{2,1,0:T(8,128)S(1)}, u32[]{:S(2)}, u32[]{:S(2)}) collective-permute-start(f32[6,128,128]{2,1,0:T(8,128)S(1)} %get-tuple-element.81), channel_id=1, source_target_pairs={{16,0},{17,1},{18,2},{19,3},{20,4},{21,5},{22,6},{23,7},{24,8},{25... | collective-permute-start | bytes 1179656 | tf_op jit(solution)/shard_map/ppermute | solution.py:10
  231.2 21.0 %collective-permute-start.2 = (f32[6,128,128]{2,1,0:T(8,128)S(1)}, f32[6,128,128]{2,1,0:T(8,128)}, u32[]{:S(2)}, u32[]{:S(2)}) collective-permute-start(f32[6,128,128]{2,1,0:T(8,128)S(1)} %get-tuple-element.80), channel_id=1, source_target_pairs={{8,0},{9,1},{10,2},{11,3},{12,4},{13,5},{14,6},{15,7},{16,8},{17,9... | collective-permute-start | bytes 1179656 | tf_op jit(solution)/shard_map/ppermute | solution.py:10
  253.3 0.7 copy-start.6
  254.1 208.8 %all-reduce.15.cloned.1.call-start = ((), (), s32[]{:S(2)}) async-start(), calls=%async_computation.3 | async-start | bytes 524288 | tf_op jit(solution)/shard_map/psum | solution.py:15
  397.8 235.9 %all-reduce.17.cloned.1.call-start = ((), (), s32[]{:S(2)}) async-start(), calls=%async_computation.4 | async-start | bytes 524288 | tf_op jit(solution)/shard_map/psum | solution.py:57
  463.9 17.2 %collective-permute-start.3 = (f32[6,128,128]{2,1,0:T(8,128)}, f32[6,128,128]{2,1,0:T(8,128)S(1)}, u32[]{:S(2)}, u32[]{:S(2)}) collective-permute-start(f32[6,128,128]{2,1,0:T(8,128)} %get-tuple-element.76), channel_id=1, source_target_pairs={{24,0},{25,1},{26,2},{27,3},{28,4},{29,5},{30,6},{31,7},{0,8},{1,9... | collective-permute-start | bytes 1179656 | tf_op jit(solution)/shard_map/ppermute | solution.py:10
  472.1 17.3 %collective-permute-start.4 = (f32[6,128,128]{2,1,0:T(8,128)S(1)}, f32[6,128,128]{2,1,0:T(8,128)S(1)}, u32[]{:S(2)}, u32[]{:S(2)}) collective-permute-start(f32[6,128,128]{2,1,0:T(8,128)S(1)} %get-tuple-element.78), channel_id=1, source_target_pairs={{16,0},{17,1},{18,2},{19,3},{20,4},{21,5},{22,6},{23,7},{24,8},{25... | collective-permute-start | bytes 1179656 | tf_op jit(solution)/shard_map/ppermute | solution.py:10
  472.1 18.2 %collective-permute-start.5 = (f32[6,128,128]{2,1,0:T(8,128)S(1)}, f32[6,128,128]{2,1,0:T(8,128)}, u32[]{:S(2)}, u32[]{:S(2)}) collective-permute-start(f32[6,128,128]{2,1,0:T(8,128)S(1)} %get-tuple-element.77), channel_id=1, source_target_pairs={{8,0},{9,1},{10,2},{11,3},{12,4},{13,5},{14,6},{15,7},{16,8},{17,9... | collective-permute-start | bytes 1179656 | tf_op jit(solution)/shard_map/ppermute | solution.py:10
  491.4 0.7 copy-start.7
  492.2 209.9 %all-reduce.19.cloned.1.call-start = ((), (), s32[]{:S(2)}) async-start(), calls=%async_computation.5 | async-start | bytes 524288 | tf_op jit(solution)/shard_map/psum | solution.py:15
  637.0 237.1 %all-reduce.21.cloned.1.call-start = ((), (), s32[]{:S(2)}) async-start(), calls=%async_computation.6 | async-start | bytes 524288 | tf_op jit(solution)/shard_map/psum | solution.py:57
  703.1 12.3 %collective-permute-start.6 = (f32[6,128,128]{2,1,0:T(8,128)}, f32[6,128,128]{2,1,0:T(8,128)S(1)}, u32[]{:S(2)}, u32[]{:S(2)}) collective-permute-start(f32[6,128,128]{2,1,0:T(8,128)} %get-tuple-element.73), channel_id=1, source_target_pairs={{24,0},{25,1},{26,2},{27,3},{28,4},{29,5},{30,6},{31,7},{0,8},{1,9... | collective-permute-start | bytes 1179656 | tf_op jit(solution)/shard_map/ppermute | solution.py:10
  704.3 26.8 %collective-permute-start.7 = (f32[6,128,128]{2,1,0:T(8,128)S(1)}, f32[6,128,128]{2,1,0:T(8,128)S(1)}, u32[]{:S(2)}, u32[]{:S(2)}) collective-permute-start(f32[6,128,128]{2,1,0:T(8,128)S(1)} %get-tuple-element.75), channel_id=1, source_target_pairs={{16,0},{17,1},{18,2},{19,3},{20,4},{21,5},{22,6},{23,7},{24,8},{25... | collective-permute-start | bytes 1179656 | tf_op jit(solution)/shard_map/ppermute | solution.py:10
  712.9 18.2 %collective-permute-start.8 = (f32[6,128,128]{2,1,0:T(8,128)S(1)}, f32[6,128,128]{2,1,0:T(8,128)}, u32[]{:S(2)}, u32[]{:S(2)}) collective-permute-start(f32[6,128,128]{2,1,0:T(8,128)S(1)} %get-tuple-element.74), channel_id=1, source_target_pairs={{8,0},{9,1},{10,2},{11,3},{12,4},{13,5},{14,6},{15,7},{16,8},{17,9... | collective-permute-start | bytes 1179656 | tf_op jit(solution)/shard_map/ppermute | solution.py:10
  732.2 0.7 copy-start.4
  733.0 209.5 %all-reduce.23.cloned.1.call-start = ((), (), s32[]{:S(2)}) async-start(), calls=%async_computation.7 | async-start | bytes 524288 | tf_op jit(solution)/shard_map/psum | solution.py:15
  942.7 11.1 %copy-start = (f32[512,128]{0,1:T(8,128)S(1)}, f32[512,128]{0,1:T(8,128)}, u32[]{:S(2)}) copy-start(f32[512,128]{0,1:T(8,128)} %all-reduce.11.cloned.1.call-done) | copy-start | bytes 786436
  942.7 11.1 %copy-start.1 = (f32[512,128]{0,1:T(8,128)S(1)}, f32[512,128]{0,1:T(8,128)}, u32[]{:S(2)}) copy-start(f32[512,128]{0,1:T(8,128)} %all-reduce.15.cloned.1.call-done) | copy-start | bytes 786436
  942.7 11.1 %copy-start.2 = (f32[512,128]{0,1:T(8,128)S(1)}, f32[512,128]{0,1:T(8,128)}, u32[]{:S(2)}) copy-start(f32[512,128]{0,1:T(8,128)} %all-reduce.19.cloned.1.call-done) | copy-start | bytes 786436
  942.7 11.1 %copy-start.3 = (f32[512,128]{0,1:T(8,128)S(1)}, f32[512,128]{0,1:T(8,128)}, u32[]{:S(2)}) copy-start(f32[512,128]{0,1:T(8,128)} %all-reduce.23.cloned.1.call-done) | copy-start | bytes 786436
  943.8 12.7 %collective-permute-start.10 = (f32[6,128,128]{2,1,0:T(8,128)}, f32[6,128,128]{2,1,0:T(8,128)}, u32[]{:S(2)}, u32[]{:S(2)}) collective-permute-start(f32[6,128,128]{2,1,0:T(8,128)} %get-tuple-element.72), channel_id=1, source_target_pairs={{16,0},{17,1},{18,2},{19,3},{20,4},{21,5},{22,6},{23,7},{24,8},{25... | collective-permute-start | bytes 1179656 | tf_op jit(solution)/shard_map/ppermute | solution.py:10
  946.5 25.5 %collective-permute-start.11 = (f32[6,128,128]{2,1,0:T(8,128)}, f32[6,128,128]{2,1,0:T(8,128)}, u32[]{:S(2)}, u32[]{:S(2)}) collective-permute-start(f32[6,128,128]{2,1,0:T(8,128)} %get-tuple-element.71), channel_id=1, source_target_pairs={{8,0},{9,1},{10,2},{11,3},{12,4},{13,5},{14,6},{15,7},{16,8},{17,9... | collective-permute-start | bytes 1179656 | tf_op jit(solution)/shard_map/ppermute | solution.py:10
  953.2 18.8 %collective-permute-start.9 = (f32[6,128,128]{2,1,0:T(8,128)}, f32[6,128,128]{2,1,0:T(8,128)}, u32[]{:S(2)}, u32[]{:S(2)}) collective-permute-start(f32[6,128,128]{2,1,0:T(8,128)} %get-tuple-element.70), channel_id=1, source_target_pairs={{24,0},{25,1},{26,2},{27,3},{28,4},{29,5},{30,6},{31,7},{0,8},{1,9... | collective-permute-start | bytes 1179656 | tf_op jit(solution)/shard_map/ppermute | solution.py:10
Sparse Core Ops, SparseCore 0:
  12.0 142.6 all-reduce.8
  158.1 64.9 all-reduce.10
  254.2 140.2 all-reduce.12
  397.9 64.9 all-reduce.14
  492.3 141.3 all-reduce.16
  637.1 64.9 all-reduce.18
  733.1 140.9 all-reduce.20
  877.5 64.9 all-reduce.22
where the time goes:
time: 981 us
  waiting for transfers between devices  890 us (91%)
  starting transfers between devices  35.4 us (4%)
  matrix products  20.2 us (2%)
  between operations  14.4 us (1%)
  local copies, waits for them, and re-layouts  14.3 us (1%)
    psum x4, waiting for transfers between devices, on_device(): complete = lax.psum(contrib, 'col')  562 us
    psum x4, waiting for transfers between devices, broadcast(): return lax.psum(jnp.where(mine, x, jnp.zeros_like(x)), axis)  260 us
    ppermute x12, waiting for transfers between devices, shifted(): return lax.ppermute(block, axis, route)  67.6 us
    ppermute x12, starting transfers between devices, shifted(): return lax.ppermute(block, axis, route)  35.1 us
  transfers between devices with their start and end apart: 20, of which 17 were waited for; matrix products, arithmetic and copies ran while one was open for 1% of the time, Pallas kernels for 0%

commit v1 on v0

--- a/solution.py
+++ b/solution.py
@@ -54,7 +54,11 @@
         contrib = placed
         is_owner = jnp.logical_and(row_pos == owner_row, group == owner_group)
         contrib = jnp.where(is_owner, contrib, jnp.zeros_like(contrib))
-        complete = lax.psum(contrib, "col")
+        complete = contrib
+        for hop in (1, 2, 4, 8, 16):
+            complete = complete + lax.ppermute(
+                complete, "col", [(dev, dev ^ hop) for dev in range(32)]
+            )
         solved_block = jnp.dot(inverses[k], complete, precision=lax.Precision.HIGHEST)
         solved_block = broadcast(solved_block, "row", owner_row)
         solved_list.append(solved_block)

time: 981 us -> 635 us (0.65)
  waiting for transfers between devices: 890 us -> 475 us
  starting transfers between devices: 35.4 us -> 97.1 us
    psum x4 -> x0, waiting for transfers between devices: 562 us -> none  [on_device(): complete = lax.psum(contrib, 'col')]
    ppermute x0 -> x20, waiting for transfers between devices: none -> 139 us  [on_device(): lax.ppermute(complete, 'col', [(dev, dev ^ hop) for dev in range(32)])]
    ppermute x0 -> x20, starting transfers between devices: none -> 61.2 us  [on_device(): lax.ppermute(complete, 'col', [(dev, dev ^ hop) for dev in range(32)])]
  transfers between devices with their start and end apart: 20 -> 36, of which waited for: 17 -> 32; matrix products, arithmetic and copies ran while one was open for 1% -> 1% of each run, Pallas kernels for 0% -> 0%
where the time goes in v1:
time: 635 us; the launch traced here: 626 us
  waiting for transfers between devices  475 us (75%)
  starting transfers between devices  97.1 us (15%)
  matrix products  19.9 us (3%)
  between operations  14.5 us (2%)
  local copies, waits for them, and re-layouts  11.5 us (2%)
  other arithmetic  7.63 us (1%)
    psum x4, waiting for transfers between devices, broadcast(): return lax.psum(jnp.where(mine, x, jnp.zeros_like(x)), axis)  268 us
    ppermute x20, waiting for transfers between devices, on_device(): lax.ppermute(complete, 'col', [(dev, dev ^ hop) for dev in range(32)])  139 us
    ppermute x12, waiting for transfers between devices, shifted(): return lax.ppermute(block, axis, route)  67.6 us
    ppermute x20, starting transfers between devices, on_device(): lax.ppermute(complete, 'col', [(dev, dev ^ hop) for dev in range(32)])  61.2 us
    ppermute x12, starting transfers between devices, shifted(): return lax.ppermute(block, axis, route)  35.7 us
    dot_general x4, matrix products, on_device(): jnp.dot(inverses[k], complete, precision=lax.Precision.HIGHEST)  12.7 us
  transfers between devices with their start and end apart: 36, of which 32 were waited for; matrix products, arithmetic and copies ran while one was open for 1% of the time, Pallas kernels for 0%

profile of v1, /device:TPU:7, one launch (start us, length us, event | category | flops | bytes accessed | tf_op | source)
XLA Modules:
  0.0 625.8 jit_solution(10397072337889971793)
XLA Ops:
  19.6 11.3 %collective-permute-done.1 = f32[512,128]{1,0:T(8,128)S(1)} collective-permute-done((f32[512,128]{1,0:T(8,128)S(1)}, f32[512,128]{1,0:T(8,128)S(1)}, u32[]{:S(2)}, u32[]{:S(2)}) %collective-permute-start.1) | collective-permute-done | bytes 262176 | tf_op jit(solution)/shard_map/ppermute | solution.py:59
  31.0 6.5 %collective-permute-start.2 = (f32[512,128]{1,0:T(8,128)S(1)}, f32[512,128]{1,0:T(8,128)S(1)}, u32[]{:S(2)}, u32[]{:S(2)}) collective-permute-start(f32[512,128]{1,0:T(8,128)S(1)} %add.236), channel_id=1, source_target_pairs={{0,4},{1,5},{2,6},{3,7},{4,0},{5,1},{6,2},{7,3},{8,12},{9,13},{10,... | collective-permute-start | bytes 786440 | tf_op jit(solution)/shard_map/ppermute | solution.py:59
  37.5 8.6 %collective-permute-done.2 = f32[512,128]{1,0:T(8,128)S(1)} collective-permute-done((f32[512,128]{1,0:T(8,128)S(1)}, f32[512,128]{1,0:T(8,128)S(1)}, u32[]{:S(2)}, u32[]{:S(2)}) %collective-permute-start.2) | collective-permute-done | bytes 262176 | tf_op jit(solution)/shard_map/ppermute | solution.py:59
  54.5 6.6 %copy.5 = f32[6,1,1,512,512]{3,4,0,2,1:T(8,128)} copy(f32[6,1,1,512,512]{4,3,2,1,0:T(8,128)} %param.11) | data formatting | bytes 12582912 | tf_op args[0]
  64.3 68.1 %all-reduce.5.cloned.1.call-done = f32[512,128]{0,1:T(8,128)} async-done(((f32[512,128]{0,1:T(8,128)}), f32[512,128]{0,1:T(8,128)}) %all-reduce.5.cloned.1.call-update) | async-done | bytes 262160 | tf_op jit(solution)/shard_map/psum | solution.py:15
  132.4 7.2 %conditional.4 = (f32[6,4,128,128]{3,2,1,0:T(8,128)S(1)}) conditional(s32[]{:T(128)} %convert_element_type.52, () %tuple.40, (f32[6,512,512]{1,2,0:T(8,128)}, f32[512,128]{0,1:T(8,128)}, f32[6,1,1]{0,2,1:T(1,128)S(1)}) %tuple.81), branch_computations={%region_1.2_spmd, %region_2.3_spmd} | conditional | flops 2416312320 | bytes 8126496 | solution.py:76
  132.4 7.2 %convolution_multiply_fusion = f32[6,512,128]{2,1,0:T(8,128)S(1)} fusion(f32[6,512,512]{1,2,0:T(8,128)} %get-tuple-element.40, f32[6]{0:T(128)S(1)} %bitcast.149, f32[512,128]{0,1:T(8,128)} %get-tuple-element.55), kind=kOutput, calls=%fused_computation | convolution fusion | flops 2416312320 | bytes 8126488 | tf_op jit(solution)/shard_map/cond/branch_1_fun/rji,jh->rih/dot_general | solution.py:69
  143.2 18.1 %collective-permute-done.5 = f32[6,128,128]{2,1,0:T(8,128)S(1)} collective-permute-done((f32[6,128,128]{2,1,0:T(8,128)}, f32[6,128,128]{2,1,0:T(8,128)S(1)}, u32[]{:S(2)}, u32[]{:S(2)}) %collective-permute-start.5) | collective-permute-done | bytes 393248 | tf_op jit(solution)/shard_map/ppermute | solution.py:10
  172.1 11.4 %collective-permute-done.9 = f32[512,128]{1,0:T(8,128)S(1)} collective-permute-done((f32[512,128]{1,0:T(8,128)S(1)}, f32[512,128]{1,0:T(8,128)S(1)}, u32[]{:S(2)}, u32[]{:S(2)}) %collective-permute-start.9) | collective-permute-done | bytes 262176 | tf_op jit(solution)/shard_map/ppermute | solution.py:59
  183.6 6.4 %collective-permute-start.10 = (f32[512,128]{1,0:T(8,128)S(1)}, f32[512,128]{1,0:T(8,128)S(1)}, u32[]{:S(2)}, u32[]{:S(2)}) collective-permute-start(f32[512,128]{1,0:T(8,128)S(1)} %add.258), channel_id=1, source_target_pairs={{0,4},{1,5},{2,6},{3,7},{4,0},{5,1},{6,2},{7,3},{8,12},{9,13},{10,... | collective-permute-start | bytes 786440 | tf_op jit(solution)/shard_map/ppermute | solution.py:59
  190.0 8.8 %collective-permute-done.10 = f32[512,128]{1,0:T(8,128)S(1)} collective-permute-done((f32[512,128]{1,0:T(8,128)S(1)}, f32[512,128]{1,0:T(8,128)S(1)}, u32[]{:S(2)}, u32[]{:S(2)}) %collective-permute-start.10) | collective-permute-done | bytes 262176 | tf_op jit(solution)/shard_map/ppermute | solution.py:59
  206.5 7.3 %collective-permute-done.12 = f32[512,128]{1,0:T(8,128)S(1)} collective-permute-done((f32[512,128]{1,0:T(8,128)S(1)}, f32[512,128]{1,0:T(8,128)S(1)}, u32[]{:S(2)}, u32[]{:S(2)}) %collective-permute-start.12) | collective-permute-done | bytes 262176 | tf_op jit(solution)/shard_map/ppermute | solution.py:59
  217.1 66.9 %all-reduce.7.cloned.1.call-done = f32[512,128]{0,1:T(8,128)} async-done(((f32[512,128]{0,1:T(8,128)}), f32[512,128]{0,1:T(8,128)}) %all-reduce.7.cloned.1.call-update) | async-done | bytes 262160 | tf_op jit(solution)/shard_map/psum | solution.py:15
  285.0 8.2 %collective-permute-start.13 = (f32[6,128,128]{2,1,0:T(8,128)}, f32[6,128,128]{2,1,0:T(8,128)S(1)}, u32[]{:S(2)}, u32[]{:S(2)}) collective-permute-start(f32[6,128,128]{2,1,0:T(8,128)} %get-tuple-element.76), channel_id=1, source_target_pairs={{24,0},{25,1},{26,2},{27,3},{28,4},{29,5},{30,6},{31,7},{0,8},{1,9... | collective-permute-start | bytes 1179656 | tf_op jit(solution)/shard_map/ppermute | solution.py:10
  295.6 6.6 %collective-permute-done.13 = f32[6,128,128]{2,1,0:T(8,128)S(1)} collective-permute-done((f32[6,128,128]{2,1,0:T(8,128)}, f32[6,128,128]{2,1,0:T(8,128)S(1)}, u32[]{:S(2)}, u32[]{:S(2)}) %collective-permute-start.13) | collective-permute-done | bytes 393248 | tf_op jit(solution)/shard_map/ppermute | solution.py:10
  302.2 8.3 %collective-permute-done.14 = f32[6,128,128]{2,1,0:T(8,128)S(1)} collective-permute-done((f32[6,128,128]{2,1,0:T(8,128)S(1)}, f32[6,128,128]{2,1,0:T(8,128)S(1)}, u32[]{:S(2)}, u32[]{:S(2)}) %collective-permute-start.14) | collective-permute-done | bytes 393248 | tf_op jit(solution)/shard_map/ppermute | solution.py:10
  313.9 6.2 collective-permute-done.16
  322.5 11.4 %collective-permute-done.17 = f32[512,128]{1,0:T(8,128)S(1)} collective-permute-done((f32[512,128]{1,0:T(8,128)S(1)}, f32[512,128]{1,0:T(8,128)S(1)}, u32[]{:S(2)}, u32[]{:S(2)}) %collective-permute-start.17) | collective-permute-done | bytes 262176 | tf_op jit(solution)/shard_map/ppermute | solution.py:59
  333.9 6.5 %collective-permute-start.18 = (f32[512,128]{1,0:T(8,128)S(1)}, f32[512,128]{1,0:T(8,128)S(1)}, u32[]{:S(2)}, u32[]{:S(2)}) collective-permute-start(f32[512,128]{1,0:T(8,128)S(1)} %add.266), channel_id=1, source_target_pairs={{0,4},{1,5},{2,6},{3,7},{4,0},{5,1},{6,2},{7,3},{8,12},{9,13},{10,... | collective-permute-start | bytes 786440 | tf_op jit(solution)/shard_map/ppermute | solution.py:59
  340.4 8.8 %collective-permute-done.18 = f32[512,128]{1,0:T(8,128)S(1)} collective-permute-done((f32[512,128]{1,0:T(8,128)S(1)}, f32[512,128]{1,0:T(8,128)S(1)}, u32[]{:S(2)}, u32[]{:S(2)}) %collective-permute-start.18) | collective-permute-done | bytes 262176 | tf_op jit(solution)/shard_map/ppermute | solution.py:59
  355.2 6.7 %collective-permute-start.20 = (f32[512,128]{1,0:T(8,128)S(1)}, f32[512,128]{1,0:T(8,128)S(1)}, u32[]{:S(2)}, u32[]{:S(2)}) collective-permute-start(f32[512,128]{1,0:T(8,128)S(1)} %add.268), channel_id=1, source_target_pairs={{0,16},{1,17},{2,18},{3,19},{4,20},{5,21},{6,22},{7,23},{8,24},{9,... | collective-permute-start | bytes 786440 | tf_op jit(solution)/shard_map/ppermute | solution.py:59
  368.9 65.9 %all-reduce.9.cloned.1.call-done = f32[512,128]{0,1:T(8,128)} async-done(((f32[512,128]{0,1:T(8,128)}), f32[512,128]{0,1:T(8,128)}) %all-reduce.9.cloned.1.call-update) | async-done | bytes 262160 | tf_op jit(solution)/shard_map/psum | solution.py:15
  437.3 8.5 %collective-permute-start.22 = (f32[6,128,128]{2,1,0:T(8,128)S(1)}, f32[6,128,128]{2,1,0:T(8,128)S(1)}, u32[]{:S(2)}, u32[]{:S(2)}) collective-permute-start(f32[6,128,128]{2,1,0:T(8,128)S(1)} %get-tuple-element.75), channel_id=1, source_target_pairs={{16,0},{17,1},{18,2},{19,3},{20,4},{21,5},{22,6},{23,7},{24,8},{25... | collective-permute-start | bytes 1179656 | tf_op jit(solution)/shard_map/ppermute | solution.py:10
  448.4 15.7 %collective-permute-done.22 = f32[6,128,128]{2,1,0:T(8,128)S(1)} collective-permute-done((f32[6,128,128]{2,1,0:T(8,128)S(1)}, f32[6,128,128]{2,1,0:T(8,128)S(1)}, u32[]{:S(2)}, u32[]{:S(2)}) %collective-permute-start.22) | collective-permute-done | bytes 393248 | tf_op jit(solution)/shard_map/ppermute | solution.py:10
  475.2 11.4 %collective-permute-done.25 = f32[512,128]{1,0:T(8,128)S(1)} collective-permute-done((f32[512,128]{1,0:T(8,128)S(1)}, f32[512,128]{1,0:T(8,128)S(1)}, u32[]{:S(2)}, u32[]{:S(2)}) %collective-permute-start.25) | collective-permute-done | bytes 262176 | tf_op jit(solution)/shard_map/ppermute | solution.py:59
  486.6 6.5 %collective-permute-start.26 = (f32[512,128]{1,0:T(8,128)S(1)}, f32[512,128]{1,0:T(8,128)S(1)}, u32[]{:S(2)}, u32[]{:S(2)}) collective-permute-start(f32[512,128]{1,0:T(8,128)S(1)} %add.274), channel_id=1, source_target_pairs={{0,4},{1,5},{2,6},{3,7},{4,0},{5,1},{6,2},{7,3},{8,12},{9,13},{10,... | collective-permute-start | bytes 786440 | tf_op jit(solution)/shard_map/ppermute | solution.py:59
  493.1 8.8 %collective-permute-done.26 = f32[512,128]{1,0:T(8,128)S(1)} collective-permute-done((f32[512,128]{1,0:T(8,128)S(1)}, f32[512,128]{1,0:T(8,128)S(1)}, u32[]{:S(2)}, u32[]{:S(2)}) %collective-permute-start.26) | collective-permute-done | bytes 262176 | tf_op jit(solution)/shard_map/ppermute | solution.py:59
  509.8 6.5 %collective-permute-done.28 = f32[512,128]{1,0:T(8,128)S(1)} collective-permute-done((f32[512,128]{1,0:T(8,128)S(1)}, f32[512,128]{1,0:T(8,128)S(1)}, u32[]{:S(2)}, u32[]{:S(2)}) %collective-permute-start.28) | collective-permute-done | bytes 262176 | tf_op jit(solution)/shard_map/ppermute | solution.py:59
  519.5 67.2 %all-reduce.11.cloned.1.call-done = f32[512,128]{0,1:T(8,128)} async-done(((f32[512,128]{0,1:T(8,128)}), f32[512,128]{0,1:T(8,128)}) %all-reduce.11.cloned.1.call-update) | async-done | bytes 262160 | tf_op jit(solution)/shard_map/psum | solution.py:15
  589.2 9.4 %collective-permute-start.30 = (f32[6,128,128]{2,1,0:T(8,128)}, f32[6,128,128]{2,1,0:T(8,128)}, u32[]{:S(2)}, u32[]{:S(2)}) collective-permute-start(f32[6,128,128]{2,1,0:T(8,128)} %get-tuple-element.72), channel_id=1, source_target_pairs={{16,0},{17,1},{18,2},{19,3},{20,4},{21,5},{22,6},{23,7},{24,8},{25... | collective-permute-start | bytes 1179656 | tf_op jit(solution)/shard_map/ppermute | solution.py:10
  599.5 7.8 %collective-permute-done.29 = f32[6,128,128]{2,1,0:T(8,128)} collective-permute-done((f32[6,128,128]{2,1,0:T(8,128)}, f32[6,128,128]{2,1,0:T(8,128)}, u32[]{:S(2)}, u32[]{:S(2)}) %collective-permute-start.29) | collective-permute-done | bytes 393248 | tf_op jit(solution)/shard_map/ppermute | solution.py:10
  607.3 9.4 %collective-permute-done.30 = f32[6,128,128]{2,1,0:T(8,128)} collective-permute-done((f32[6,128,128]{2,1,0:T(8,128)}, f32[6,128,128]{2,1,0:T(8,128)}, u32[]{:S(2)}, u32[]{:S(2)}) %collective-permute-start.30) | collective-permute-done | bytes 393248 | tf_op jit(solution)/shard_map/ppermute | solution.py:10
  (103 shorter events, 104.6 us)
Async XLA Ops:
  7.2 125.3 %all-reduce.5.cloned.1.call-start = ((), (), s32[]{:S(2)}) async-start(), calls=%async_computation | async-start | bytes 524288 | tf_op jit(solution)/shard_map/psum | solution.py:15
  8.1 7.5 %collective-permute-start = (f32[512,128]{1,0:T(8,128)S(1)}, f32[512,128]{1,0:T(8,128)S(1)}, u32[]{:S(2)}, u32[]{:S(2)}) collective-permute-start(f32[512,128]{1,0:T(8,128)S(1)} %bitcast_dynamic-update-slice_fusion), channel_id=1, source_target_pairs={{0,1},{1,0},{2,3},{3,2},{4,5},{5,4},{6,7},{7,6},{8,9},{9,8},{10,11... | collective-permute-start | bytes 786440 | tf_op jit(solution)/shard_map/ppermute | solution.py:59
  16.5 14.4 %collective-permute-start.1 = (f32[512,128]{1,0:T(8,128)S(1)}, f32[512,128]{1,0:T(8,128)S(1)}, u32[]{:S(2)}, u32[]{:S(2)}) collective-permute-start(f32[512,128]{1,0:T(8,128)S(1)} %fusion.39), channel_id=1, source_target_pairs={{0,2},{1,3},{2,0},{3,1},{4,6},{5,7},{6,4},{7,5},{8,10},{9,11},{10,... | collective-permute-start | bytes 786440 | tf_op jit(solution)/shard_map/ppermute | solution.py:59
  31.0 15.1 %collective-permute-start.2 = (f32[512,128]{1,0:T(8,128)S(1)}, f32[512,128]{1,0:T(8,128)S(1)}, u32[]{:S(2)}, u32[]{:S(2)}) collective-permute-start(f32[512,128]{1,0:T(8,128)S(1)} %add.236), channel_id=1, source_target_pairs={{0,4},{1,5},{2,6},{3,7},{4,0},{5,1},{6,2},{7,3},{8,12},{9,13},{10,... | collective-permute-start | bytes 786440 | tf_op jit(solution)/shard_map/ppermute | solution.py:59
  51.5 9.6 %collective-permute-start.4 = (f32[512,128]{1,0:T(8,128)S(1)}, f32[512,128]{1,0:T(8,128)S(1)}, u32[]{:S(2)}, u32[]{:S(2)}) collective-permute-start(f32[512,128]{1,0:T(8,128)S(1)} %add.238), channel_id=1, source_target_pairs={{0,16},{1,17},{2,18},{3,19},{4,20},{5,21},{6,22},{7,23},{8,24},{9,... | collective-permute-start | bytes 786440 | tf_op jit(solution)/shard_map/ppermute | solution.py:59
  64.2 219.7 %all-reduce.7.cloned.1.call-start = ((), (), s32[]{:S(2)}) async-start(), calls=%async_computation.1 | async-start | bytes 524288 | tf_op jit(solution)/shard_map/psum | solution.py:15
  140.5 20.7 %collective-permute-start.5 = (f32[6,128,128]{2,1,0:T(8,128)}, f32[6,128,128]{2,1,0:T(8,128)S(1)}, u32[]{:S(2)}, u32[]{:S(2)}) collective-permute-start(f32[6,128,128]{2,1,0:T(8,128)} %get-tuple-element.79), channel_id=1, source_target_pairs={{24,0},{25,1},{26,2},{27,3},{28,4},{29,5},{30,6},{31,7},{0,8},{1,9... | collective-permute-start | bytes 1179656 | tf_op jit(solution)/shard_map/ppermute | solution.py:10
  140.5 20.7 %collective-permute-start.6 = (f32[6,128,128]{2,1,0:T(8,128)S(1)}, f32[6,128,128]{2,1,0:T(8,128)S(1)}, u32[]{:S(2)}, u32[]{:S(2)}) collective-permute-start(f32[6,128,128]{2,1,0:T(8,128)S(1)} %get-tuple-element.81), channel_id=1, source_target_pairs={{16,0},{17,1},{18,2},{19,3},{20,4},{21,5},{22,6},{23,7},{24,8},{25... | collective-permute-start | bytes 1179656 | tf_op jit(solution)/shard_map/ppermute | solution.py:10
  140.5 21.0 %collective-permute-start.7 = (f32[6,128,128]{2,1,0:T(8,128)S(1)}, f32[6,128,128]{2,1,0:T(8,128)}, u32[]{:S(2)}, u32[]{:S(2)}) collective-permute-start(f32[6,128,128]{2,1,0:T(8,128)S(1)} %get-tuple-element.80), channel_id=1, source_target_pairs={{8,0},{9,1},{10,2},{11,3},{12,4},{13,5},{14,6},{15,7},{16,8},{17,9... | collective-permute-start | bytes 1179656 | tf_op jit(solution)/shard_map/ppermute | solution.py:10
  162.7 7.1 %collective-permute-start.8 = (f32[512,128]{1,0:T(8,128)S(1)}, f32[512,128]{1,0:T(8,128)S(1)}, u32[]{:S(2)}, u32[]{:S(2)}) collective-permute-start(f32[512,128]{1,0:T(8,128)S(1)} %fusion.40), channel_id=1, source_target_pairs={{0,1},{1,0},{2,3},{3,2},{4,5},{5,4},{6,7},{7,6},{8,9},{9,8},{10,11... | collective-permute-start | bytes 786440 | tf_op jit(solution)/shard_map/ppermute | solution.py:59
  169.7 13.8 %collective-permute-start.9 = (f32[512,128]{1,0:T(8,128)S(1)}, f32[512,128]{1,0:T(8,128)S(1)}, u32[]{:S(2)}, u32[]{:S(2)}) collective-permute-start(f32[512,128]{1,0:T(8,128)S(1)} %add_dynamic-update-slice_fusion.2), channel_id=1, source_target_pairs={{0,2},{1,3},{2,0},{3,1},{4,6},{5,7},{6,4},{7,5},{8,10},{9,11},{10,... | collective-permute-start | bytes 786440 | tf_op jit(solution)/shard_map/ppermute | solution.py:59
  183.6 15.2 %collective-permute-start.10 = (f32[512,128]{1,0:T(8,128)S(1)}, f32[512,128]{1,0:T(8,128)S(1)}, u32[]{:S(2)}, u32[]{:S(2)}) collective-permute-start(f32[512,128]{1,0:T(8,128)S(1)} %add.258), channel_id=1, source_target_pairs={{0,4},{1,5},{2,6},{3,7},{4,0},{5,1},{6,2},{7,3},{8,12},{9,13},{10,... | collective-permute-start | bytes 786440 | tf_op jit(solution)/shard_map/ppermute | solution.py:59
  204.3 9.5 %collective-permute-start.12 = (f32[512,128]{1,0:T(8,128)S(1)}, f32[512,128]{1,0:T(8,128)S(1)}, u32[]{:S(2)}, u32[]{:S(2)}) collective-permute-start(f32[512,128]{1,0:T(8,128)S(1)} %add.260), channel_id=1, source_target_pairs={{0,16},{1,17},{2,18},{3,19},{4,20},{5,21},{6,22},{7,23},{8,24},{9,... | collective-permute-start | bytes 786440 | tf_op jit(solution)/shard_map/ppermute | solution.py:59
  217.0 217.8 %all-reduce.9.cloned.1.call-start = ((), (), s32[]{:S(2)}) async-start(), calls=%async_computation.2 | async-start | bytes 524288 | tf_op jit(solution)/shard_map/psum | solution.py:15
  285.0 17.2 %collective-permute-start.13 = (f32[6,128,128]{2,1,0:T(8,128)}, f32[6,128,128]{2,1,0:T(8,128)S(1)}, u32[]{:S(2)}, u32[]{:S(2)}) collective-permute-start(f32[6,128,128]{2,1,0:T(8,128)} %get-tuple-element.76), channel_id=1, source_target_pairs={{24,0},{25,1},{26,2},{27,3},{28,4},{29,5},{30,6},{31,7},{0,8},{1,9... | collective-permute-start | bytes 1179656 | tf_op jit(solution)/shard_map/ppermute | solution.py:10
  293.2 17.3 %collective-permute-start.14 = (f32[6,128,128]{2,1,0:T(8,128)S(1)}, f32[6,128,128]{2,1,0:T(8,128)S(1)}, u32[]{:S(2)}, u32[]{:S(2)}) collective-permute-start(f32[6,128,128]{2,1,0:T(8,128)S(1)} %get-tuple-element.78), channel_id=1, source_target_pairs={{16,0},{17,1},{18,2},{19,3},{20,4},{21,5},{22,6},{23,7},{24,8},{25... | collective-permute-start | bytes 1179656 | tf_op jit(solution)/shard_map/ppermute | solution.py:10
  293.2 18.2 %collective-permute-start.15 = (f32[6,128,128]{2,1,0:T(8,128)S(1)}, f32[6,128,128]{2,1,0:T(8,128)}, u32[]{:S(2)}, u32[]{:S(2)}) collective-permute-start(f32[6,128,128]{2,1,0:T(8,128)S(1)} %get-tuple-element.77), channel_id=1, source_target_pairs={{8,0},{9,1},{10,2},{11,3},{12,4},{13,5},{14,6},{15,7},{16,8},{17,9... | collective-permute-start | bytes 1179656 | tf_op jit(solution)/shard_map/ppermute | solution.py:10
  312.5 7.6 %collective-permute-start.16 = (f32[512,128]{1,0:T(8,128)S(1)}, f32[512,128]{1,0:T(8,128)S(1)}, u32[]{:S(2)}, u32[]{:S(2)}) collective-permute-start(f32[512,128]{1,0:T(8,128)S(1)} %fusion.41), channel_id=1, source_target_pairs={{0,1},{1,0},{2,3},{3,2},{4,5},{5,4},{6,7},{7,6},{8,9},{9,8},{10,11... | collective-permute-start | bytes 786440 | tf_op jit(solution)/shard_map/ppermute | solution.py:59
  320.1 13.8 %collective-permute-start.17 = (f32[512,128]{1,0:T(8,128)S(1)}, f32[512,128]{1,0:T(8,128)S(1)}, u32[]{:S(2)}, u32[]{:S(2)}) collective-permute-start(f32[512,128]{1,0:T(8,128)S(1)} %add_dynamic-update-slice_fusion.1), channel_id=1, source_target_pairs={{0,2},{1,3},{2,0},{3,1},{4,6},{5,7},{6,4},{7,5},{8,10},{9,11},{10,... | collective-permute-start | bytes 786440 | tf_op jit(solution)/shard_map/ppermute | solution.py:59
  333.9 15.3 %collective-permute-start.18 = (f32[512,128]{1,0:T(8,128)S(1)}, f32[512,128]{1,0:T(8,128)S(1)}, u32[]{:S(2)}, u32[]{:S(2)}) collective-permute-start(f32[512,128]{1,0:T(8,128)S(1)} %add.266), channel_id=1, source_target_pairs={{0,4},{1,5},{2,6},{3,7},{4,0},{5,1},{6,2},{7,3},{8,12},{9,13},{10,... | collective-permute-start | bytes 786440 | tf_op jit(solution)/shard_map/ppermute | solution.py:59
  355.2 10.5 %collective-permute-start.20 = (f32[512,128]{1,0:T(8,128)S(1)}, f32[512,128]{1,0:T(8,128)S(1)}, u32[]{:S(2)}, u32[]{:S(2)}) collective-permute-start(f32[512,128]{1,0:T(8,128)S(1)} %add.268), channel_id=1, source_target_pairs={{0,16},{1,17},{2,18},{3,19},{4,20},{5,21},{6,22},{7,23},{8,24},{9,... | collective-permute-start | bytes 786440 | tf_op jit(solution)/shard_map/ppermute | solution.py:59
  368.9 217.8 %all-reduce.11.cloned.1.call-start = ((), (), s32[]{:S(2)}) async-start(), calls=%async_computation.3 | async-start | bytes 524288 | tf_op jit(solution)/shard_map/psum | solution.py:15
  436.1 12.3 %collective-permute-start.21 = (f32[6,128,128]{2,1,0:T(8,128)}, f32[6,128,128]{2,1,0:T(8,128)S(1)}, u32[]{:S(2)}, u32[]{:S(2)}) collective-permute-start(f32[6,128,128]{2,1,0:T(8,128)} %get-tuple-element.73), channel_id=1, source_target_pairs={{24,0},{25,1},{26,2},{27,3},{28,4},{29,5},{30,6},{31,7},{0,8},{1,9... | collective-permute-start | bytes 1179656 | tf_op jit(solution)/shard_map/ppermute | solution.py:10
  437.3 26.8 %collective-permute-start.22 = (f32[6,128,128]{2,1,0:T(8,128)S(1)}, f32[6,128,128]{2,1,0:T(8,128)S(1)}, u32[]{:S(2)}, u32[]{:S(2)}) collective-permute-start(f32[6,128,128]{2,1,0:T(8,128)S(1)} %get-tuple-element.75), channel_id=1, source_target_pairs={{16,0},{17,1},{18,2},{19,3},{20,4},{21,5},{22,6},{23,7},{24,8},{25... | collective-permute-start | bytes 1179656 | tf_op jit(solution)/shard_map/ppermute | solution.py:10
  445.8 18.2 %collective-permute-start.23 = (f32[6,128,128]{2,1,0:T(8,128)S(1)}, f32[6,128,128]{2,1,0:T(8,128)}, u32[]{:S(2)}, u32[]{:S(2)}) collective-permute-start(f32[6,128,128]{2,1,0:T(8,128)S(1)} %get-tuple-element.74), channel_id=1, source_target_pairs={{8,0},{9,1},{10,2},{11,3},{12,4},{13,5},{14,6},{15,7},{16,8},{17,9... | collective-permute-start | bytes 1179656 | tf_op jit(solution)/shard_map/ppermute | solution.py:10
  465.2 7.6 %collective-permute-start.24 = (f32[512,128]{1,0:T(8,128)S(1)}, f32[512,128]{1,0:T(8,128)S(1)}, u32[]{:S(2)}, u32[]{:S(2)}) collective-permute-start(f32[512,128]{1,0:T(8,128)S(1)} %fusion.42), channel_id=1, source_target_pairs={{0,1},{1,0},{2,3},{3,2},{4,5},{5,4},{6,7},{7,6},{8,9},{9,8},{10,11... | collective-permute-start | bytes 786440 | tf_op jit(solution)/shard_map/ppermute | solution.py:59
  472.8 13.8 %collective-permute-start.25 = (f32[512,128]{1,0:T(8,128)S(1)}, f32[512,128]{1,0:T(8,128)S(1)}, u32[]{:S(2)}, u32[]{:S(2)}) collective-permute-start(f32[512,128]{1,0:T(8,128)S(1)} %add_dynamic-update-slice_fusion), channel_id=1, source_target_pairs={{0,2},{1,3},{2,0},{3,1},{4,6},{5,7},{6,4},{7,5},{8,10},{9,11},{10,... | collective-permute-start | bytes 786440 | tf_op jit(solution)/shard_map/ppermute | solution.py:59
  486.6 15.3 %collective-permute-start.26 = (f32[512,128]{1,0:T(8,128)S(1)}, f32[512,128]{1,0:T(8,128)S(1)}, u32[]{:S(2)}, u32[]{:S(2)}) collective-permute-start(f32[512,128]{1,0:T(8,128)S(1)} %add.274), channel_id=1, source_target_pairs={{0,4},{1,5},{2,6},{3,7},{4,0},{5,1},{6,2},{7,3},{8,12},{9,13},{10,... | collective-permute-start | bytes 786440 | tf_op jit(solution)/shard_map/ppermute | solution.py:59
  507.3 8.9 %collective-permute-start.28 = (f32[512,128]{1,0:T(8,128)S(1)}, f32[512,128]{1,0:T(8,128)S(1)}, u32[]{:S(2)}, u32[]{:S(2)}) collective-permute-start(f32[512,128]{1,0:T(8,128)S(1)} %add.276), channel_id=1, source_target_pairs={{0,16},{1,17},{2,18},{3,19},{4,20},{5,21},{6,22},{7,23},{8,24},{9,... | collective-permute-start | bytes 786440 | tf_op jit(solution)/shard_map/ppermute | solution.py:59
  588.0 19.4 %collective-permute-start.29 = (f32[6,128,128]{2,1,0:T(8,128)}, f32[6,128,128]{2,1,0:T(8,128)}, u32[]{:S(2)}, u32[]{:S(2)}) collective-permute-start(f32[6,128,128]{2,1,0:T(8,128)} %get-tuple-element.70), channel_id=1, source_target_pairs={{24,0},{25,1},{26,2},{27,3},{28,4},{29,5},{30,6},{31,7},{0,8},{1,9... | collective-permute-start | bytes 1179656 | tf_op jit(solution)/shard_map/ppermute | solution.py:10
  589.2 27.6 %collective-permute-start.30 = (f32[6,128,128]{2,1,0:T(8,128)}, f32[6,128,128]{2,1,0:T(8,128)}, u32[]{:S(2)}, u32[]{:S(2)}) collective-permute-start(f32[6,128,128]{2,1,0:T(8,128)} %get-tuple-element.72), channel_id=1, source_target_pairs={{16,0},{17,1},{18,2},{19,3},{20,4},{21,5},{22,6},{23,7},{24,8},{25... | collective-permute-start | bytes 1179656 | tf_op jit(solution)/shard_map/ppermute | solution.py:10
  598.6 18.2 %collective-permute-start.31 = (f32[6,128,128]{2,1,0:T(8,128)}, f32[6,128,128]{2,1,0:T(8,128)}, u32[]{:S(2)}, u32[]{:S(2)}) collective-permute-start(f32[6,128,128]{2,1,0:T(8,128)} %get-tuple-element.71), channel_id=1, source_target_pairs={{8,0},{9,1},{10,2},{11,3},{12,4},{13,5},{14,6},{15,7},{16,8},{17,9... | collective-permute-start | bytes 1179656 | tf_op jit(solution)/shard_map/ppermute | solution.py:10
  (9 other events, 90.9 us)
Sparse Core Ops, SparseCore 0:
  64.4 68.0 all-reduce.4
  217.1 66.7 all-reduce.6
  369.0 65.8 all-reduce.8
  519.6 67.0 all-reduce.10
